TPU v7x, 256 devices: a whole 4x4x8 slice. The times are simulated.
256 devices in a mesh: seq: 128 (over y_hi, x, z, core), chan: 2 (over y_lo).
Axes of the slice: x: 4, y: 4 (y_hi: 2, y_lo: 2; y = y_hi * 2 + y_lo), z: 8, core: 2. Of those that a mesh axis runs over, the one named last changes fastest.
Arguments:
- tokens: bfloat16 [262144, 1024], P('seq', 'chan'), may hold values from -6 to 6
- w_gate: bfloat16 [1024, 1024], P(None, 'chan'), may hold values from -0.1875 to 0.1875
- w_value: bfloat16 [1024, 1024], P(None, 'chan'), may hold values from -0.1875 to 0.1875
- row_mix: bfloat16 [512, 512], replicated, may hold values from -0.25 to 0.25
- col_mix: bfloat16 [512, 512], replicated, may hold values from -0.25 to 0.25
- kernel: bfloat16 [512, 512, 1024], P(None, 'seq', 'chan'), may hold values from -6 to 6
- cotangent: bfloat16 [262144, 1024], P('seq', 'chan'), may hold values from -6 to 6
Outputs:
- grad_tokens: bfloat16 [262144, 1024], P('seq', 'chan')
- grad_kernel: bfloat16 [512, 512, 1024], P(None, 'seq', 'chan')
All inputs are finite; a program needn't handle non-finite values.
Results may differ from a plain program's by a relative error of at most 0.009.
Values may be sent and summed in bfloat16 or wider, within the bound.
A program may use at most 128 MiB of HBM per device.

v0:
```python
import jax
import jax.numpy as jnp
from jax import lax
from jax.sharding import PartitionSpec as P

N2 = 512


def rounded(values):
    return lax.optimization_barrier(values.astype(jnp.bfloat16))


def contract_last(left, right):
    return lax.dot_general(
        left, right, (((1,), (1,)), ((), ())), preferred_element_type=jnp.float32
    )


def body(tokens, w_gate, w_value, row_mix, col_mix, kernel, cotangent):
    tok_rows, local = tokens.shape
    grid_rows = tok_rows // N2
    piece = lax.all_gather(tokens, "chan", axis=1, tiled=True)
    gate_sum = jnp.dot(piece, w_gate, preferred_element_type=jnp.float32)
    value_sum = jnp.dot(piece, w_value, preferred_element_type=jnp.float32)
    gate = rounded(gate_sum)
    value = value_sum.astype(jnp.bfloat16)
    value_grid = value.reshape(grid_rows, N2, local)
    row_mixed = jnp.einsum(
        "ijc,jk->ikc", value_grid, row_mix, preferred_element_type=jnp.float32
    ).astype(jnp.bfloat16)
    columns = jnp.einsum(
        "im,ikc->mkc",
        col_mix,
        lax.all_to_all(row_mixed, "seq", split_axis=1, concat_axis=0, tiled=True),
        preferred_element_type=jnp.float32,
    ).astype(jnp.bfloat16)
    columns = lax.optimization_barrier(columns)
    kernel_wide = kernel.astype(jnp.float32)
    spectrum = rounded(kernel_wide * columns.astype(jnp.float32))
    mixed = lax.all_to_all(spectrum, "seq", split_axis=0, concat_axis=1, tiled=True).reshape(
        tok_rows, local
    )
    upstream = cotangent.astype(jnp.float32)
    grad_gate = rounded(upstream * mixed.astype(jnp.float32))
    grad_mixed = (
        (upstream * gate.astype(jnp.float32)).astype(jnp.bfloat16).reshape(grid_rows, N2, local)
    )
    grad_spectrum = lax.all_to_all(grad_mixed, "seq", split_axis=1, concat_axis=0, tiled=True)
    grad_wide = grad_spectrum.astype(jnp.float32)
    grad_kernel = (grad_wide * columns.astype(jnp.float32)).astype(jnp.bfloat16)
    grad_columns = (grad_wide * kernel_wide).astype(jnp.bfloat16)
    grad_rows = jnp.einsum(
        "im,mkc->ikc", col_mix, grad_columns, preferred_element_type=jnp.float32
    ).astype(jnp.bfloat16)
    grad_value = (
        jnp.einsum(
            "ikc,jk->ijc",
            lax.all_to_all(grad_rows, "seq", split_axis=0, concat_axis=1, tiled=True),
            row_mix,
            preferred_element_type=jnp.float32,
        )
        .astype(jnp.bfloat16)
        .reshape(tok_rows, local)
    )
    terms = contract_last(grad_gate, w_gate) + contract_last(grad_value, w_value)
    grad_tokens = lax.psum_scatter(
        terms.astype(jnp.bfloat16), "chan", scatter_dimension=1, tiled=True
    )
    return (grad_tokens, grad_kernel)


def solution(mesh):
    in_specs = (
        P("seq", "chan"),
        P(None, "chan"),
        P(None, "chan"),
        P(),
        P(),
        P(None, "seq", "chan"),
        P("seq", "chan"),
    )
    out_specs = (P("seq", "chan"), P(None, "seq", "chan"))
    return jax.shard_map(body, mesh=mesh, in_specs=in_specs, out_specs=out_specs, check_vma=False)
```

profile of v0, /device:TPU:14, one launch (start us, length us, event | category | flops | bytes accessed | tf_op | source)
XLA Modules:
  0.0 411.4 jit_solution(15781595476893682583)
XLA Ops:
  7.2 0.0 copy-start
  7.2 0.0 all-gather.2.cloned.1.call-start
  7.2 0.7 all-gather.2.cloned.1.call-update
  7.9 0.0 copy-start.3
  7.9 65.6 %all-gather.2.cloned.1.call-done = bf16[2048,1024]{1,0:T(8,128)(2,1)} async-done(((bf16[2048,512]{1,0:T(8,128)(2,1)}), bf16[2048,1024]{1,0:T(8,128)(2,1)}) %all-gather.2.cloned.1.call-update) | async-done | bytes 4194320 | tf_op jit(solution)/shard_map/all_gather | solution.py:22
  73.5 4.5 %convolution_convert_fusion = bf16[2048,512]{1,0:T(8,128)(2,1)S(1)} fusion(bf16[2048,1024]{1,0:T(8,128)(2,1)} %all-gather.2.cloned.1.call-done, bf16[1024,512]{1,0:T(8,128)(2,1)S(1)} %copy-done), kind=kOutput, calls=%fused_computation.13 | convolution fusion | flops 2148532224 | bytes 7340032 | tf_op jit(solution)/shard_map/dot_general | solution.py:23
  78.0 0.6 fusion.1
  78.6 2.9 copy.36
  81.6 13.4 %all-to-all-start.2 = ((bf16[4,512,512]{2,0,1:T(4,128)(2,1)}), bf16[4,512,512]{2,0,1:T(4,128)(2,1)S(1)}, u32[]{:S(2)}, u32[]{:S(2)}) async-start(bf16[4,512,512]{2,0,1:T(4,128)(2,1)} %copy.36), calls=%async_computation.2 | async-start | bytes 4194304 | tf_op jit(solution)/shard_map/all_to_all | solution.py:48
  94.9 0.0 copy-start.8
  95.0 4.9 %convolution_convert_fusion.1 = bf16[2048,512]{1,0:T(8,128)(2,1)S(1)} fusion(bf16[2048,1024]{1,0:T(8,128)(2,1)} %all-gather.2.cloned.1.call-done, bf16[1024,512]{1,0:T(8,128)(2,1)} %param.9), kind=kOutput, calls=%fused_computation.14 | convolution fusion | flops 2148532224 | bytes 7340032 | tf_op jit(solution)/shard_map/dot_general | solution.py:24
  99.8 2.6 convert_bitcast_fusion.4
  102.5 4.5 %copy.31 = bf16[4,512,512]{2,0,1:T(4,128)(2,1)} copy(bf16[4,512,512]{1,2,0:T(8,128)(2,1)} %convert_bitcast_fusion.4) | data formatting | bytes 4194304 | tf_op jit(solution)/shard_map/convert_element_type | solution.py:30
  107.0 38.1 %all-to-all-done.2 = bf16[4,512,512]{2,0,1:T(4,128)(2,1)S(1)} async-done(((bf16[4,512,512]{2,0,1:T(4,128)(2,1)}), bf16[4,512,512]{2,0,1:T(4,128)(2,1)S(1)}, u32[]{:S(2)}, u32[]{:S(2)}) %all-to-all-start.2) | async-done | bytes 2097184 | tf_op jit(solution)/shard_map/all_to_all | solution.py:48
  145.1 1.3 copy-done.2
  146.4 10.8 %all-to-all-start = ((bf16[4,512,512]{2,0,1:T(4,128)(2,1)}), bf16[4,512,512]{2,0,1:T(4,128)(2,1)}, u32[]{:S(2)}, u32[]{:S(2)}) async-start(bf16[4,512,512]{2,0,1:T(4,128)(2,1)} %copy.31), calls=%async_computation | async-start | bytes 4194304 | tf_op jit(solution)/shard_map/all_to_all | solution.py:34
  157.2 3.0 copy.29
  160.2 2.3 convert_bitcast_fusion
  162.5 4.0 copy.37
  166.5 5.2 %copy.38 = f32[512,4,512]{0,2,1:T(8,128)} copy(f32[512,4,512]{2,1,0:T(4,128)} %bitcast.47) | data formatting | bytes 8388608 | tf_op jit(solution)/shard_map/convert_element_type | solution.py:49
  171.8 4.9 %convert_bitcast_fusion.2 = bf16[512,4,512]{0,2,1:T(8,128)(2,1)} fusion(f32[512,4,512]{0,2,1:T(8,128)} %copy.38, bf16[512,4,512]{0,2,1:T(8,128)(2,1)S(1)} %copy.29, bf16[512,512]{1,0:T(8,128)(2,1)} %param.11), kind=kOutput, calls=%fused_computation.18 | convolution fusion | flops 1077936128 | bytes 8912896 | tf_op jit(solution)/shard_map/im,mkc->ikc/dot_general | solution.py:52
  176.7 4.5 %copy.39 = bf16[512,4,512]{2,1,0:T(4,128)(2,1)} copy(bf16[512,4,512]{0,2,1:T(8,128)(2,1)} %convert_bitcast_fusion.2) | data formatting | bytes 4194304 | tf_op jit(solution)/shard_map/convert_element_type | solution.py:54
  181.2 25.8 %all-to-all-done = bf16[4,512,512]{2,0,1:T(4,128)(2,1)} async-done(((bf16[4,512,512]{2,0,1:T(4,128)(2,1)}), bf16[4,512,512]{2,0,1:T(4,128)(2,1)}, u32[]{:S(2)}, u32[]{:S(2)}) %all-to-all-start) | async-done | bytes 2097184 | tf_op jit(solution)/shard_map/all_to_all | solution.py:34
  207.0 10.8 %all-to-all-start.3 = ((bf16[512,4,512]{2,1,0:T(4,128)(2,1)}), bf16[512,4,512]{2,1,0:T(4,128)(2,1)}, u32[]{:S(2)}, u32[]{:S(2)}) async-start(bf16[512,4,512]{2,1,0:T(4,128)(2,1)} %copy.39), calls=%async_computation.3 | async-start | bytes 4194304 | tf_op jit(solution)/shard_map/all_to_all | solution.py:58
  217.8 0.0 copy-start.6
  217.9 2.9 copy.32
  220.8 1.4 convert_bitcast_fusion.3
  222.1 0.8 copy-done.1
  222.9 3.0 fusion.4
  226.0 4.5 %copy.34 = bf16[512,4,512]{2,1,0:T(4,128)(2,1)} copy(bf16[512,4,512]{0,2,1:T(8,128)(2,1)} %get-tuple-element.9) | data formatting | bytes 4194304 | tf_op jit(solution)/shard_map/optimization_barrier | solution.py:10
  230.5 37.1 %all-to-all-done.3 = bf16[512,4,512]{2,1,0:T(4,128)(2,1)} async-done(((bf16[512,4,512]{2,1,0:T(4,128)(2,1)}), bf16[512,4,512]{2,1,0:T(4,128)(2,1)}, u32[]{:S(2)}, u32[]{:S(2)}) %all-to-all-start.3) | async-done | bytes 2097184 | tf_op jit(solution)/shard_map/all_to_all | solution.py:58
  267.6 10.4 %all-to-all-start.1 = ((bf16[512,4,512]{2,1,0:T(4,128)(2,1)}), bf16[512,4,512]{2,1,0:T(4,128)(2,1)S(1)}, u32[]{:S(2)}, u32[]{:S(2)}) async-start(bf16[512,4,512]{2,1,0:T(4,128)(2,1)} %copy.34), calls=%async_computation.1 | async-start | bytes 4194304 | tf_op jit(solution)/shard_map/all_to_all | solution.py:40
  278.0 0.0 reduce-scatter.2.cloned.1.call-start
  278.1 3.6 copy.40
  281.7 4.0 all_to_all.49
  285.6 4.3 %convolution_convert_fusion.2 = bf16[4,512,512]{1,2,0:T(8,128)(2,1)} fusion(bf16[4,512,512]{2,1,0:T(8,128)(2,1)} %all_to_all.49, bf16[512,512]{1,0:T(8,128)(2,1)} %param.10), kind=kOutput, calls=%fused_computation.21 | convolution fusion | flops 1074790400 | bytes 4718592 | tf_op jit(solution)/shard_map/ikc,jk->ijc/dot_general | solution.py:56
  290.0 38.1 %all-to-all-done.1 = bf16[512,4,512]{2,1,0:T(4,128)(2,1)S(1)} async-done(((bf16[512,4,512]{2,1,0:T(4,128)(2,1)}), bf16[512,4,512]{2,1,0:T(4,128)(2,1)S(1)}, u32[]{:S(2)}, u32[]{:S(2)}) %all-to-all-start.1) | async-done | bytes 2097184 | tf_op jit(solution)/shard_map/all_to_all | solution.py:40
  328.1 0.7 convert_bitcast_fusion.1
  328.8 2.7 copy.35
  331.6 5.5 %reshape.26 = f32[2048,512]{1,0:T(8,128)} reshape(f32[4,128,4,512]{3,2,1,0:T(4,128)} %copy.35) | data formatting | bytes 8388608 | tf_op jit(solution)/shard_map/convert_element_type | solution.py:44
  337.1 2.9 fusion
  340.0 0.0 copy-start.9
  340.0 2.4 fusion.17
  342.4 4.4 %add_convert_fusion = bf16[2048,1024]{1,0:T(8,128)(2,1)} fusion(f32[2048,1024]{1,0:T(8,128)S(1)} %fusion.17, bf16[2048,512]{1,0:T(8,128)(2,1)S(1)} %bitcast.52, bf16[1024,512]{1,0:T(8,128)(2,1)S(1)} %copy-done.7), kind=kOutput, calls=%fused_computation | convolution fusion | flops 2151677952 | bytes 15728640 | tf_op jit(solution)/shard_map/dot_general | solution.py:14
  346.8 0.0 reduce-scatter.2.cloned.1.call-update
  346.9 1.6 copy-done.5
  348.4 3.1 copy.42
  351.5 53.0 %reduce-scatter.2.cloned.1.call-done = bf16[2048,512]{1,0:T(8,128)(2,1)} async-done(((bf16[2048,1024]{1,0:T(8,128)(2,1)}), bf16[2048,512]{1,0:T(8,128)(2,1)}) %reduce-scatter.2.cloned.1.call-update) | async-done | bytes 2097168 | tf_op jit(solution)/shard_map/reduce_scatter | solution.py:66
  (12 shorter events, 0.0 us)
Async XLA Ops:
  7.2 66.3 %copy-start = (bf16[1024,512]{1,0:T(8,128)(2,1)S(1)}, bf16[1024,512]{1,0:T(8,128)(2,1)}, u32[]{:S(2)}) copy-start(bf16[1024,512]{1,0:T(8,128)(2,1)} %param.8) | copy-start | bytes 3145732
  7.2 66.3 %all-gather.2.cloned.1.call-start = ((), (), s32[]{:S(2)}) async-start(), calls=%async_computation.5 | async-start | bytes 6291456 | tf_op jit(solution)/shard_map/all_gather | solution.py:22
  7.9 70.1 %copy-start.3 = (bf16[2048,512]{1,0:T(8,128)(2,1)S(1)}, bf16[2048,512]{1,0:T(8,128)(2,1)}, u32[]{:S(2)}) copy-start(bf16[2048,512]{1,0:T(8,128)(2,1)} %param.13) | copy-start | bytes 6291460
  81.6 63.5 %all-to-all-start.2 = ((bf16[4,512,512]{2,0,1:T(4,128)(2,1)}), bf16[4,512,512]{2,0,1:T(4,128)(2,1)S(1)}, u32[]{:S(2)}, u32[]{:S(2)}) async-start(bf16[4,512,512]{2,0,1:T(4,128)(2,1)} %copy.36), calls=%async_computation.2 | async-start | bytes 4194304 | tf_op jit(solution)/shard_map/all_to_all | solution.py:48
  94.9 4.9 %copy-start.8 = (bf16[512,512]{1,0:T(8,128)(2,1)S(1)}, bf16[512,512]{1,0:T(8,128)(2,1)}, u32[]{:S(2)}) copy-start(bf16[512,512]{1,0:T(8,128)(2,1)} %param.10) | copy-start | bytes 1572868
  145.1 1.3 copy-start.2
  146.4 60.6 %all-to-all-start = ((bf16[4,512,512]{2,0,1:T(4,128)(2,1)}), bf16[4,512,512]{2,0,1:T(4,128)(2,1)}, u32[]{:S(2)}, u32[]{:S(2)}) async-start(bf16[4,512,512]{2,0,1:T(4,128)(2,1)} %copy.31), calls=%async_computation | async-start | bytes 4194304 | tf_op jit(solution)/shard_map/all_to_all | solution.py:34
  207.0 60.6 %all-to-all-start.3 = ((bf16[512,4,512]{2,1,0:T(4,128)(2,1)}), bf16[512,4,512]{2,1,0:T(4,128)(2,1)}, u32[]{:S(2)}, u32[]{:S(2)}) async-start(bf16[512,4,512]{2,1,0:T(4,128)(2,1)} %copy.39), calls=%async_computation.3 | async-start | bytes 4194304 | tf_op jit(solution)/shard_map/all_to_all | solution.py:58
  217.8 2.9 copy-start.6
  220.7 2.2 copy-start.1
  267.6 60.5 %all-to-all-start.1 = ((bf16[512,4,512]{2,1,0:T(4,128)(2,1)}), bf16[512,4,512]{2,1,0:T(4,128)(2,1)S(1)}, u32[]{:S(2)}, u32[]{:S(2)}) async-start(bf16[512,4,512]{2,1,0:T(4,128)(2,1)} %copy.34), calls=%async_computation.1 | async-start | bytes 4194304 | tf_op jit(solution)/shard_map/all_to_all | solution.py:40
  278.0 126.5 %reduce-scatter.2.cloned.1.call-start = ((), (), s32[]{:S(2)}) async-start(), calls=%async_computation.6 | async-start | bytes 6291456 | tf_op jit(solution)/shard_map/reduce_scatter | solution.py:66
  331.6 5.5 %copy-start.4 = (bf16[2048,512]{1,0:T(8,128)(2,1)S(1)}, bf16[2048,512]{1,0:T(8,128)(2,1)}, u32[]{:S(2)}) copy-start(bf16[2048,512]{1,0:T(8,128)(2,1)} %param.13) | copy-start | bytes 6291460
  340.0 2.4 copy-start.7
  340.0 2.4 copy-start.9
  346.8 1.6 copy-start.5
Sparse Core Ops, SparseCore 0:
  9.8 63.6 all-gather.1
  347.0 57.4 reduce-scatter.1
where the time goes:
time: 414 us; the launch traced here: 411 us
  waiting for transfers between devices  258 us (62%)
  local copies, waits for them, and re-layouts  54.3 us (13%)
  starting transfers between devices  45.5 us (11%)
  matrix products  29.4 us (7%)
  between operations  14.2 us (3%)
  other arithmetic  9.48 us (2%)
    all_gather x1, waiting for transfers between devices, body(): piece = lax.all_gather(tokens, 'chan', axis=1, tiled=True)  65.6 us
    reduce_scatter x1, waiting for transfers between devices, body(): lax.psum_scatter(terms.astype(jnp.bfloat16), 'chan', scatter_dimension=1,...  53 us
    all_to_all x1, waiting for transfers between devices, body(): lax.all_to_all(spectrum, 'seq', split_axis=0, concat_axis=1, tiled=True)  38.1 us
    all_to_all x1, waiting for transfers between devices, body(): lax.all_to_all(grad_mixed, 'seq', split_axis=1, concat_axis=0, tiled=True)  38.1 us
    all_to_all x1, waiting for transfers between devices, body(): lax.all_to_all(grad_rows, 'seq', split_axis=0, concat_axis=1, tiled=True)  37.1 us
    all_to_all x1, waiting for transfers between devices, body(): lax.all_to_all(row_mixed, 'seq', split_axis=1, concat_axis=0, tiled=True)  25.8 us
    all_to_all x1, starting transfers between devices, body(): lax.all_to_all(grad_mixed, 'seq', split_axis=1, concat_axis=0, tiled=True)  13.4 us
    all_to_all x1, starting transfers between devices, body(): lax.all_to_all(row_mixed, 'seq', split_axis=1, concat_axis=0, tiled=True)  10.8 us
  transfers between devices with their start and end apart: 6, of which 6 were waited for; matrix products, arithmetic and copies ran while one was open for 14% of the time, Pallas kernels for 0%

commit v1 on v0

v1 whole, which is shorter than its diff:
```python
import jax
import jax.numpy as jnp
from jax import lax
from jax.experimental import pallas as pl
from jax.experimental.pallas import tpu as pltpu
from jax.sharding import PartitionSpec as P

MESH = pl.DeviceIdType.MESH
F32 = jnp.float32
BF16 = jnp.bfloat16
Q = 4
BLK = 32


def mm(left, right):
    return jnp.dot(left, right, preferred_element_type=F32)


def mm_nt(left, right):
    return lax.dot_general(left, right, (((1,), (1,)), ((), ())), preferred_element_type=F32)


def selection(rows, cols, column_of):
    row = lax.broadcasted_iota(jnp.int32, (rows, cols), 0)
    col = lax.broadcasted_iota(jnp.int32, (rows, cols), 1)
    return jnp.where(col == column_of(row), 1.0, 0.0).astype(BF16)


def make_kernel(n, side, local):
    half = side // 2
    lanes = min(256, local)

    def kernel(
        tok_h, wg_h, wv_h, rm_h, cm_h, ker_h, cot_h,
        gt_h, gk_h,
        tok, tokp, wg, wv, rm, rmt, cm, cmp, cmpt, perm, regroup, ungroup,
        ker, cot, sa, ra, sb, rb, pin, gcol, gk, stack, rss, rsr, own, out,
        in_sem, self_sem, ag_s, ag_r, a_s, a_r, b_s, b_r, rs_s, rs_r, gt_sem, gk_sem,
    ):
        me = lax.axis_index("seq")
        ch = lax.axis_index("chan")
        other = 1 - ch

        loads = [
            pltpu.make_async_copy(src, dst, in_sem.at[at])
            for at, (src, dst) in enumerate(
                (
                    (cm_h, cm), (rm_h, rm), (wv_h, wv), (tok_h, tok),
                    (wg_h, wg), (cot_h, cot), (ker_h, ker),
                )
            )
        ]
        for load in loads:
            load.start()

        barrier = pltpu.get_barrier_semaphore()

        def greet(step, carry):
            pl.semaphore_signal(
                barrier, inc=1, device_id={"seq": lax.rem(me + step, n)}, device_id_type=MESH
            )
            return carry

        pl.semaphore_signal(barrier, inc=1, device_id={"chan": other}, device_id_type=MESH)
        lax.fori_loop(1, n, greet, 0)
        pl.semaphore_wait(barrier, n)

        def gather(i):
            return pltpu.make_async_remote_copy(
                src_ref=tok_h.at[i],
                dst_ref=tokp.at[i],
                send_sem=ag_s.at[i],
                recv_sem=ag_r.at[i],
                device_id={"chan": other},
                device_id_type=MESH,
            )

        for i in range(Q):
            gather(i).start()

        perm[...] = selection(side, side, lambda r: Q * lax.rem(r, n) + r // n)
        regroup[...] = selection(8 * BLK, 8 * BLK, lambda r: lax.rem(r, BLK) * 8 + r // BLK)
        ungroup[...] = selection(8 * BLK, 8 * BLK, lambda r: lax.rem(r, 8) * BLK + r // 8)
        loads[0].wait()
        cmp[...] = mm(perm[...], cm[...]).astype(BF16)
        cmpt[...] = mm_nt(perm[...], cm[...]).astype(BF16)
        cmp[...] = mm_nt(cmp[...], perm[...]).astype(BF16)
        cmpt[...] = mm_nt(cmpt[...], perm[...]).astype(BF16)
        loads[1].wait()
        rmt[...] = mm_nt(selection(side, side, lambda r: r), rm[...]).astype(BF16)
        for load in loads[2:]:
            load.wait()

        low = lax.broadcasted_iota(jnp.int32, (side // 8, 8, lanes), 1) < 4

        def exchange(src, dst, i, send_sem, recv_sem, self_at):
            def push(step, carry):
                to = lax.rem(me + step, n)
                pltpu.make_async_remote_copy(
                    src_ref=src.at[i, to],
                    dst_ref=dst.at[i, me],
                    send_sem=send_sem.at[i],
                    recv_sem=recv_sem.at[i],
                    device_id={"seq": to},
                    device_id_type=MESH,
                ).start()
                return carry

            lax.fori_loop(1, n, push, 0)
            pltpu.make_async_copy(src.at[i, me], dst.at[i, me], self_sem.at[self_at]).start()

        def arrived(src, dst, i, recv_sem, self_at):
            pltpu.make_async_copy(
                dst.at[i, pl.ds(0, n - 1)], dst.at[i, pl.ds(0, n - 1)], recv_sem.at[i]
            ).wait()
            pltpu.make_async_copy(src.at[i, me], dst.at[i, me], self_sem.at[self_at]).wait()

        def sent(src, i, send_sem):
            pltpu.make_async_copy(
                src.at[i, pl.ds(0, n - 1)], src.at[i, pl.ds(0, n - 1)], send_sem.at[i]
            ).wait()

        def tokens_step(i, carry):
            gather(i).wait_recv()

            def part(b, inner):
                cols = pl.ds(pl.multiple_of(b * lanes, lanes), lanes)
                mine, theirs = tok[i], tokp[i]
                value = (mm(mine, wv[ch, :, cols]) + mm(theirs, wv[other, :, cols])).astype(BF16)
                rows = mm(rmt[...], value).reshape(side // 8, 8, lanes)
                gate = (mm(mine, wg[ch, :, cols]) + mm(theirs, wg[other, :, cols])).astype(BF16)
                grad = (cot[i, :, cols].astype(F32) * gate.astype(F32)).reshape(side // 8, 8, lanes)
                even = jnp.where(low, rows, pltpu.roll(grad, 4, 1))
                odd = jnp.where(low, pltpu.roll(rows, 4, 1), grad)
                both = jnp.stack([even, odd], axis=1).reshape(n, 8, lanes)
                sa[i, :, :, cols] = both.astype(BF16)
                return inner

            lax.fori_loop(0, local // lanes, part, 0)
            exchange(sa, ra, i, a_s, a_r, i)
            return carry

        lax.fori_loop(0, Q, tokens_step, 0)

        def planes_step(i, carry):
            arrived(sa, ra, i, a_r, i)

            def block(b, inner):
                start = pl.multiple_of(b * BLK, BLK)
                tile = ra[i, pl.ds(start, BLK)].astype(F32).reshape(8 * BLK, local).astype(BF16)
                moved = mm(regroup[...], tile).astype(BF16).reshape(8, BLK, local)
                rows = pl.ds(pl.multiple_of(i * n + start, BLK), BLK)
                pin[:, rows, :] = moved
                gcol[:, rows, :] = (
                    moved[4:].astype(F32) * ker[:, rows, :].astype(F32)
                ).astype(BF16)
                return inner

            lax.fori_loop(0, n // BLK, block, 0)
            return carry

        lax.fori_loop(0, Q, planes_step, 0)

        def columns_step(i, carry):
            rows = pl.ds(pl.multiple_of(i * n, n), n)

            def plane(k, inner):
                columns = mm(cmpt[rows, :], pin[k]).astype(BF16).astype(F32)
                stack[k] = (ker[k, rows, :].astype(F32) * columns).astype(BF16)
                gk[k, rows, :] = (pin[Q + k, rows, :].astype(F32) * columns).astype(BF16)
                stack[Q + k] = mm(cmp[rows, :], gcol[k]).astype(BF16)
                return inner

            lax.fori_loop(0, Q, plane, 0)

            def block(b, inner):
                start = pl.multiple_of(b * BLK, BLK)
                tile = stack[:, pl.ds(start, BLK), :].reshape(8 * BLK, local)
                sb[i, pl.ds(start, BLK)] = (
                    mm(ungroup[...], tile).reshape(BLK, 8, local).astype(BF16)
                )
                return inner

            lax.fori_loop(0, n // BLK, block, 0)
            exchange(sb, rb, i, b_s, b_r, Q + i)
            return carry

        lax.fori_loop(0, Q, columns_step, 0)

        store_gk = pltpu.make_async_copy(gk, gk_h, gk_sem)
        store_gk.start()

        def scatter(i):
            return pltpu.make_async_remote_copy(
                src_ref=rss.at[i],
                dst_ref=rsr.at[i],
                send_sem=rs_s.at[i],
                recv_sem=rs_r.at[i],
                device_id={"chan": other},
                device_id_type=MESH,
            )

        def store(i):
            return pltpu.make_async_copy(out.at[i], gt_h.at[i], gt_sem.at[i])

        def finish(i):
            scatter(i).wait_recv()
            out[i] = (own[i] + rsr[i].astype(F32)).astype(BF16)
            store(i).start()

        def rows_step(i, carry):
            arrived(sb, rb, i, b_r, Q + i)

            def part(b, inner):
                cols = pl.ds(pl.multiple_of(b * lanes, lanes), lanes)
                tiles = rb[i, :, :, cols].astype(F32).reshape(n // 2, 2, 8, lanes)
                even, odd = tiles[:, 0], tiles[:, 1]
                mixed = jnp.where(low, even, pltpu.roll(odd, 4, 1)).reshape(side, lanes)
                grad = jnp.where(low, pltpu.roll(even, 4, 1), odd).reshape(side, lanes)
                tok[i, :, cols] = (cot[i, :, cols].astype(F32) * mixed).astype(BF16)
                tokp[i, :, cols] = mm(rm[...], grad.astype(BF16)).astype(BF16)
                return inner

            lax.fori_loop(0, local // lanes, part, 0)

            def away(b, inner):
                rows = pl.ds(pl.multiple_of(b * lanes, lanes), lanes)
                rss[i, :, rows] = (
                    mm_nt(tok[i], wg[other, rows, :]) + mm_nt(tokp[i], wv[other, rows, :])
                ).astype(BF16)
                return inner

            lax.fori_loop(0, local // lanes, away, 0)
            scatter(i).start()

            def home(b, inner):
                rows = pl.ds(pl.multiple_of(b * lanes, lanes), lanes)
                own[i, :, rows] = mm_nt(tok[i], wg[ch, rows, :]) + mm_nt(tokp[i], wv[ch, rows, :])
                return inner

            lax.fori_loop(0, local // lanes, home, 0)

            @pl.when(i > 0)
            def _():
                finish(i - 1)

            return carry

        lax.fori_loop(0, Q, rows_step, 0)
        finish(Q - 1)

        for i in range(Q):
            gather(i).wait_send()
            sent(sa, i, a_s)
            sent(sb, i, b_s)
            scatter(i).wait_send()
            store(i).wait()
        store_gk.wait()

    return kernel


def body(tokens, w_gate, w_value, row_mix, col_mix, kernel, cotangent):
    n = lax.axis_size("seq")
    side, local = row_mix.shape[0], tokens.shape[1]
    planes = kernel.reshape(n, Q, Q, local).transpose(2, 1, 0, 3).reshape(Q, side, local)
    anywhere = pl.BlockSpec(memory_space=pl.ANY)
    wide = (Q, side, local)
    tiles = (Q, n, 8, local)
    square = (side, side)
    dma = pltpu.SemaphoreType.DMA
    grad_tokens, grad_planes = pl.pallas_call(
        make_kernel(n, side, local),
        name="monarch_backward",
        out_shape=(jax.ShapeDtypeStruct(wide, BF16), jax.ShapeDtypeStruct(wide, BF16)),
        in_specs=[anywhere] * 7,
        out_specs=(anywhere, anywhere),
        scratch_shapes=[
            pltpu.VMEM(wide, BF16), pltpu.VMEM(wide, BF16),
            pltpu.VMEM((2, local, local), BF16), pltpu.VMEM((2, local, local), BF16),
            *[pltpu.VMEM(square, BF16) for _ in range(6)],
            pltpu.VMEM((8 * BLK, 8 * BLK), BF16), pltpu.VMEM((8 * BLK, 8 * BLK), BF16),
            pltpu.VMEM(wide, BF16), pltpu.VMEM(wide, BF16),
            *[pltpu.VMEM(tiles, BF16) for _ in range(4)],
            pltpu.VMEM((2 * Q, side, local), BF16),
            pltpu.VMEM(wide, BF16), pltpu.VMEM(wide, BF16),
            pltpu.VMEM((2 * Q, n, local), BF16),
            pltpu.VMEM(wide, BF16), pltpu.VMEM(wide, BF16),
            pltpu.VMEM(wide, F32), pltpu.VMEM(wide, BF16),
            dma((7,)), dma((2 * Q,)),
            *[dma((Q,)) for _ in range(9)],
            dma,
        ],
        compiler_params=pltpu.CompilerParams(
            collective_id=0, has_side_effects=True, vmem_limit_bytes=66_000_000
        ),
    )(
        tokens.reshape(wide),
        w_gate.reshape(2, local, local),
        w_value.reshape(2, local, local),
        row_mix,
        col_mix,
        planes,
        cotangent.reshape(wide),
    )
    grad_kernel = (
        grad_planes.reshape(Q, Q, n, local).transpose(2, 1, 0, 3).reshape(side, Q, local)
    )
    return grad_tokens.reshape(Q * side, local), grad_kernel


def solution(mesh):
    in_specs = (
        P("seq", "chan"),
        P(None, "chan"),
        P(None, "chan"),
        P(),
        P(),
        P(None, "seq", "chan"),
        P("seq", "chan"),
    )
    out_specs = (P("seq", "chan"), P(None, "seq", "chan"))
    return jax.shard_map(body, mesh=mesh, in_specs=in_specs, out_specs=out_specs, check_vma=False)
```

time: 414 us -> 247 us (0.60)
  waiting for transfers between devices: 258 us -> 0 us
  Pallas kernels: 0 us -> 236 us
  starting transfers between devices: 45.5 us -> 0 us
  local copies, waits for them, and re-layouts: 54.3 us -> 10.1 us
  matrix products: 29.4 us -> 0 us
  between operations: 14.2 us -> 0.65 us
  other arithmetic: 9.48 us -> 0 us
    pallas_call x0 -> x1, Pallas kernels: none -> 236 us  [body(): pl.pallas_call(make_kernel(n, side, local), name='monarch_backward', out_...]
    all_to_all x4 -> x0, waiting for transfers between devices: 139 us -> none  [the longest x1 38.1 us: body(): lax.all_to_all(spectrum, 'seq', split_axis=0, concat_axis=1, tiled=True)]
    all_gather x1 -> x0, waiting for transfers between devices: 65.6 us -> none  [body(): piece = lax.all_gather(tokens, 'chan', axis=1, tiled=True)]
    reduce_scatter x1 -> x0, waiting for transfers between devices: 53 us -> none  [body(): lax.psum_scatter(terms.astype(jnp.bfloat16), 'chan', scatter_dimension=1,...]
    all_to_all x4 -> x0, starting transfers between devices: 45.4 us -> none  [the longest x1 13.4 us: body(): lax.all_to_all(grad_mixed, 'seq', split_axis=1, concat_axis=0, tiled=True)]
    dot_general x8 -> x0, matrix products: 29.4 us -> none  [the longest x2 6.81 us: contract_last(): lax.dot_general(left, right, (((1,), (1,)), ((), ())), preferred_element_...]
    convert_element_type x6 -> x0, local copies, waits for them, and re-layouts: 26.6 us -> none  [the longest x2 9.27 us: body(): grad_wide = grad_spectrum.astype(jnp.float32)]
    all_to_all x3 -> x0, local copies, waits for them, and re-layouts: 10.4 us -> none  [the longest x2 7.58 us: body(): lax.all_to_all(grad_rows, 'seq', split_axis=0, concat_axis=1, tiled=True)]
  transfers between devices with their start and end apart: 6 -> 0, of which waited for: 6 -> 0; matrix products, arithmetic and copies ran while one was open for 14% -> 0% of each run, Pallas kernels for 0% -> 0%
where the time goes in v1:
time: 247 us; the launch traced here: 246 us
  Pallas kernels  236 us (96%)
  local copies, waits for them, and re-layouts  10.1 us (4%)
    pallas_call x1, Pallas kernels, body(): pl.pallas_call(make_kernel(n, side, local), name='monarch_backward', out_...  236 us

profile of v1, /device:TPU:14, one launch (start us, length us, event | category | flops | bytes accessed | tf_op | source)
XLA Modules:
  0.0 246.5 jit_solution(7539943104938327262)
XLA Ops:
  0.6 4.1 %copy.9 = bf16[128,4,4,512]{3,0,1,2:T(8,128)(2,1)} copy(bf16[128,4,4,512]{3,2,1,0:T(4,128)(2,1)} %bitcast.14) | data formatting | bytes 4194304 | tf_op jit(solution)/shard_map/reshape | solution.py:266
  4.7 235.7 %monarch_backward.1 = (bf16[4,512,512]{2,1,0:T(8,128)(2,1)}, bf16[4,512,512]{2,1,0:T(8,128)(2,1)}) custom-call(bf16[4,512,512]{2,1,0:T(8,128)(2,1)} %bitcast.18, bf16[2,512,512]{2,1,0:T(8,128)(2,1)} %bitcast.20, bf16[2,512,512]{2,1,0:T(8,128)(2,1)} %bitcast.21, bf16[512,512]{1,0:T(8,128)(2,1)} %rm_h.1, bf16[512,512]{1,0:T(8,128)(2,1)} %cm_h.1, ...), custom_call_target="tpu_custom_call" | custom-call | tf_op jit(solution)/shard_map/monarch_backward/pallas_call | solution.py:272
  240.4 0.0 copy-start
  240.5 4.7 %copy.10 = bf16[128,4,4,512]{3,2,1,0:T(4,128)(2,1)} copy(bf16[128,4,4,512]{3,0,1,2:T(8,128)(2,1)} %bitcast.17) | data formatting | bytes 4194304 | tf_op jit(solution)/shard_map/transpose | solution.py:307
  245.1 0.0 copy-done
  245.1 1.3 copy.12
Async XLA Ops:
  240.4 4.7 %copy-start = (bf16[4,512,512]{2,1,0:T(8,128)(2,1)S(1)}, bf16[4,512,512]{2,1,0:T(8,128)(2,1)}, u32[]{:S(2)}) copy-start(bf16[4,512,512]{2,1,0:T(8,128)(2,1)} %get-tuple-element.4) | copy-start | bytes 6291460

commit v2 on v1

--- a/solution.py
+++ b/solution.py
@@ -10,6 +10,7 @@
 BF16 = jnp.bfloat16
 Q = 4
 BLK = 32
+RUN = 16
 
 
 def mm(left, right):
@@ -33,7 +34,7 @@
     def kernel(
         tok_h, wg_h, wv_h, rm_h, cm_h, ker_h, cot_h,
         gt_h, gk_h,
-        tok, tokp, wg, wv, rm, rmt, cm, cmp, cmpt, perm, regroup, ungroup,
+        tok, tokp, wg, wv, rm, rmt, cm, cmp, cmpt, perm, regroup, ungroup, split, join, raw,
         ker, cot, sa, ra, sb, rb, pin, gcol, gk, stack, rss, rsr, own, out,
         in_sem, self_sem, ag_s, ag_r, a_s, a_r, b_s, b_r, rs_s, rs_r, gt_sem, gk_sem,
     ):
@@ -46,7 +47,7 @@
             for at, (src, dst) in enumerate(
                 (
                     (cm_h, cm), (rm_h, rm), (wv_h, wv), (tok_h, tok),
-                    (wg_h, wg), (cot_h, cot), (ker_h, ker),
+                    (wg_h, wg), (cot_h, cot), (ker_h, raw),
                 )
             )
         ]
@@ -81,6 +82,14 @@
         perm[...] = selection(side, side, lambda r: Q * lax.rem(r, n) + r // n)
         regroup[...] = selection(8 * BLK, 8 * BLK, lambda r: lax.rem(r, BLK) * 8 + r // BLK)
         ungroup[...] = selection(8 * BLK, 8 * BLK, lambda r: lax.rem(r, 8) * BLK + r // 8)
+        split[...] = selection(
+            Q * Q * RUN, Q * Q * RUN,
+            lambda r: lax.rem(r, RUN) * Q * Q + lax.rem(r // RUN, Q) * Q + r // (Q * RUN),
+        )
+        join[...] = selection(
+            Q * Q * RUN, Q * Q * RUN,
+            lambda r: (lax.rem(r, Q) * Q + lax.rem(r // Q, Q)) * RUN + r // (Q * Q),
+        )
         loads[0].wait()
         cmp[...] = mm(perm[...], cm[...]).astype(BF16)
         cmpt[...] = mm_nt(perm[...], cm[...]).astype(BF16)
@@ -142,6 +151,22 @@
 
         lax.fori_loop(0, Q, tokens_step, 0)
 
+        def run(i, b):
+            return pl.ds(pl.multiple_of(i * n + b * RUN, RUN), RUN)
+
+        def positions(b):
+            return pl.ds(pl.multiple_of(b * Q * RUN, Q * RUN), Q * RUN)
+
+        def to_planes(b, carry):
+            flat = raw[positions(b)].astype(F32).reshape(Q * Q * RUN, local).astype(BF16)
+            moved = mm(split[...], flat).astype(BF16)
+            for k in range(Q):
+                for i in range(Q):
+                    ker[k, run(i, b), :] = moved[(k * Q + i) * RUN : (k * Q + i + 1) * RUN]
+            return carry
+
+        lax.fori_loop(0, n // RUN, to_planes, 0)
+
         def planes_step(i, carry):
             arrived(sa, ra, i, a_r, i)
 
@@ -187,7 +212,15 @@
 
         lax.fori_loop(0, Q, columns_step, 0)
 
-        store_gk = pltpu.make_async_copy(gk, gk_h, gk_sem)
+        def from_planes(b, carry):
+            flat = jnp.concatenate(
+                [gk[k, run(i, b), :] for k in range(Q) for i in range(Q)], axis=0
+            )
+            raw[positions(b)] = mm(join[...], flat).reshape(Q * RUN, Q, local).astype(BF16)
+            return carry
+
+        lax.fori_loop(0, n // RUN, from_planes, 0)
+        store_gk = pltpu.make_async_copy(raw, gk_h, gk_sem)
         store_gk.start()
 
         def scatter(i):
@@ -263,16 +296,17 @@
 def body(tokens, w_gate, w_value, row_mix, col_mix, kernel, cotangent):
     n = lax.axis_size("seq")
     side, local = row_mix.shape[0], tokens.shape[1]
-    planes = kernel.reshape(n, Q, Q, local).transpose(2, 1, 0, 3).reshape(Q, side, local)
     anywhere = pl.BlockSpec(memory_space=pl.ANY)
     wide = (Q, side, local)
     tiles = (Q, n, 8, local)
     square = (side, side)
     dma = pltpu.SemaphoreType.DMA
-    grad_tokens, grad_planes = pl.pallas_call(
+    grad_tokens, grad_kernel = pl.pallas_call(
         make_kernel(n, side, local),
         name="monarch_backward",
-        out_shape=(jax.ShapeDtypeStruct(wide, BF16), jax.ShapeDtypeStruct(wide, BF16)),
+        out_shape=(
+            jax.ShapeDtypeStruct(wide, BF16), jax.ShapeDtypeStruct((side, Q, local), BF16),
+        ),
         in_specs=[anywhere] * 7,
         out_specs=(anywhere, anywhere),
         scratch_shapes=[
@@ -280,6 +314,8 @@
             pltpu.VMEM((2, local, local), BF16), pltpu.VMEM((2, local, local), BF16),
             *[pltpu.VMEM(square, BF16) for _ in range(6)],
             pltpu.VMEM((8 * BLK, 8 * BLK), BF16), pltpu.VMEM((8 * BLK, 8 * BLK), BF16),
+            *[pltpu.VMEM((Q * Q * RUN, Q * Q * RUN), BF16) for _ in range(2)],
+            pltpu.VMEM((side, Q, local), BF16),
             pltpu.VMEM(wide, BF16), pltpu.VMEM(wide, BF16),
             *[pltpu.VMEM(tiles, BF16) for _ in range(4)],
             pltpu.VMEM((2 * Q, side, local), BF16),
@@ -300,11 +336,8 @@
         w_value.reshape(2, local, local),
         row_mix,
         col_mix,
-        planes,
+        kernel,
         cotangent.reshape(wide),
-    )
-    grad_kernel = (
-        grad_planes.reshape(Q, Q, n, local).transpose(2, 1, 0, 3).reshape(side, Q, local)
     )
     return grad_tokens.reshape(Q * side, local), grad_kernel
 

time: 247 us -> 241 us (0.976)
  local copies, waits for them, and re-layouts: 10.1 us -> 4.52 us
    transpose x1 -> x0, local copies, waits for them, and re-layouts: 4.68 us -> none  [body(): grad_planes.reshape(Q, Q, n, local).transpose(2, 1, 0, 3)]
    reshape x1 -> x0, local copies, waits for them, and re-layouts: 4.07 us -> none  [body(): kernel.reshape(n, Q, Q, local).transpose(2, 1, 0, 3).reshape(Q, side, local)]
    unnamed x3 -> x4, local copies, waits for them, and re-layouts: 1.32 us -> 4.52 us
where the time goes in v2:
time: 241 us
  Pallas kernels  236 us (98%)
  local copies, waits for them, and re-layouts  4.52 us (2%)
    pallas_call x1, Pallas kernels, body(): pl.pallas_call(make_kernel(n, side, local), name='monarch_backward', out_...  236 us

profile of v2, /device:TPU:14, one launch (start us, length us, event | category | flops | bytes accessed | tf_op | source)
XLA Modules:
  0.0 241.4 jit_solution(2707770613498213376)
XLA Ops:
  0.6 236.2 %monarch_backward.1 = (bf16[4,512,512]{2,1,0:T(8,128)(2,1)}, bf16[512,4,512]{2,1,0:T(4,128)(2,1)}) custom-call(bf16[4,512,512]{2,1,0:T(8,128)(2,1)} %bitcast.6, bf16[2,512,512]{2,1,0:T(8,128)(2,1)} %bitcast.8, bf16[2,512,512]{2,1,0:T(8,128)(2,1)} %bitcast.9, bf16[512,512]{1,0:T(8,128)(2,1)} %rm_h.1, bf16[512,512]{1,0:T(8,128)(2,1)} %cm_h.1, ...), custom_call_target="tpu_custom_call" | custom-call | tf_op jit(solution)/shard_map/monarch_backward/pallas_call | solution.py:304
  236.9 0.0 copy-start
  236.9 3.2 %copy.11 = bf16[2048,512]{1,0:T(8,128)(2,1)} copy(bf16[2048,512]{1,0:T(8,128)(2,1)} %bitcast.5) | data formatting | bytes 4194304
  240.1 0.0 copy-done
  240.1 1.3 copy.12
Async XLA Ops:
  236.9 3.2 %copy-start = (bf16[512,4,512]{2,1,0:T(4,128)(2,1)S(1)}, bf16[512,4,512]{2,1,0:T(4,128)(2,1)}, u32[]{:S(2)}) copy-start(bf16[512,4,512]{2,1,0:T(4,128)(2,1)} %get-tuple-element.9) | copy-start | bytes 6291460

commit v3 on v2

--- a/solution.py
+++ b/solution.py
@@ -10,6 +10,7 @@
 BF16 = jnp.bfloat16
 Q = 4
 BLK = 32
+GREET = 7
 RUN = 16
 
 
@@ -56,14 +57,18 @@
 
         barrier = pltpu.get_barrier_semaphore()
 
-        def greet(step, carry):
+        def greet(group, carry):
+            for at in range(GREET):
+                to = lax.rem(me + group * GREET + at + 1, n)
+                pl.semaphore_signal(barrier, inc=1, device_id={"seq": to}, device_id_type=MESH)
+            return carry
+
+        pl.semaphore_signal(barrier, inc=1, device_id={"chan": other}, device_id_type=MESH)
+        lax.fori_loop(0, (n - 1) // GREET, greet, 0)
+        for step in range((n - 1) // GREET * GREET + 1, n):
             pl.semaphore_signal(
                 barrier, inc=1, device_id={"seq": lax.rem(me + step, n)}, device_id_type=MESH
             )
-            return carry
-
-        pl.semaphore_signal(barrier, inc=1, device_id={"chan": other}, device_id_type=MESH)
-        lax.fori_loop(1, n, greet, 0)
         pl.semaphore_wait(barrier, n)
 
         def gather(i):
@@ -102,14 +107,14 @@
 
         low = lax.broadcasted_iota(jnp.int32, (side // 8, 8, lanes), 1) < 4
 
-        def exchange(src, dst, i, send_sem, recv_sem, self_at):
+        def exchange(src, dst, i, send_sem, landed, self_at):
             def push(step, carry):
                 to = lax.rem(me + step, n)
                 pltpu.make_async_remote_copy(
                     src_ref=src.at[i, to],
                     dst_ref=dst.at[i, me],
                     send_sem=send_sem.at[i],
-                    recv_sem=recv_sem.at[i],
+                    recv_sem=landed,
                     device_id={"seq": to},
                     device_id_type=MESH,
                 ).start()
@@ -146,7 +151,7 @@
                 return inner
 
             lax.fori_loop(0, local // lanes, part, 0)
-            exchange(sa, ra, i, a_s, a_r, i)
+            exchange(sa, ra, i, a_s, a_r.at[i, me // BLK], i)
             return carry
 
         lax.fori_loop(0, Q, tokens_step, 0)
@@ -168,9 +173,13 @@
         lax.fori_loop(0, n // RUN, to_planes, 0)
 
         def planes_step(i, carry):
-            arrived(sa, ra, i, a_r, i)
-
-            def block(b, inner):
+            mine = me // BLK
+
+            def landed(b, count):
+                some = ra.at[i, pl.ds(pl.multiple_of(b * BLK, BLK), count)]
+                pltpu.make_async_copy(some, some, a_r.at[i, b]).wait()
+
+            def block(b):
                 start = pl.multiple_of(b * BLK, BLK)
                 tile = ra[i, pl.ds(start, BLK)].astype(F32).reshape(8 * BLK, local).astype(BF16)
                 moved = mm(regroup[...], tile).astype(BF16).reshape(8, BLK, local)
@@ -179,9 +188,17 @@
                 gcol[:, rows, :] = (
                     moved[4:].astype(F32) * ker[:, rows, :].astype(F32)
                 ).astype(BF16)
-                return inner
-
-            lax.fori_loop(0, n // BLK, block, 0)
+
+            def group(step, inner):
+                b = lax.rem(mine + n // BLK - step, n // BLK)
+                landed(b, BLK)
+                block(b)
+                return inner
+
+            lax.fori_loop(1, n // BLK, group, 0)
+            landed(mine, BLK - 1)
+            pltpu.make_async_copy(sa.at[i, me], ra.at[i, me], self_sem.at[i]).wait()
+            block(mine)
             return carry
 
         lax.fori_loop(0, Q, planes_step, 0)
@@ -207,7 +224,7 @@
                 return inner
 
             lax.fori_loop(0, n // BLK, block, 0)
-            exchange(sb, rb, i, b_s, b_r, Q + i)
+            exchange(sb, rb, i, b_s, b_r.at[i], Q + i)
             return carry
 
         lax.fori_loop(0, Q, columns_step, 0)
@@ -324,7 +341,8 @@
             pltpu.VMEM(wide, BF16), pltpu.VMEM(wide, BF16),
             pltpu.VMEM(wide, F32), pltpu.VMEM(wide, BF16),
             dma((7,)), dma((2 * Q,)),
-            *[dma((Q,)) for _ in range(9)],
+            dma((Q,)), dma((Q,)), dma((Q,)), dma((Q, n // BLK)),
+            *[dma((Q,)) for _ in range(5)],
             dma,
         ],
         compiler_params=pltpu.CompilerParams(

time: 241 us -> 240 us (level)
  no operation moved by 1% of the time
where the time goes in v3:
time: 240 us
  Pallas kernels  235 us (98%)
  local copies, waits for them, and re-layouts  4.52 us (2%)
    pallas_call x1, Pallas kernels, body(): pl.pallas_call(make_kernel(n, side, local), name='monarch_backward', out_...  235 us

profile of v3, /device:TPU:14, one launch (start us, length us, event | category | flops | bytes accessed | tf_op | source)
XLA Modules:
  0.0 240.3 jit_solution(4293365441461483587)
XLA Ops:
  0.6 235.1 %monarch_backward.1 = (bf16[4,512,512]{2,1,0:T(8,128)(2,1)}, bf16[512,4,512]{2,1,0:T(4,128)(2,1)}) custom-call(bf16[4,512,512]{2,1,0:T(8,128)(2,1)} %bitcast.6, bf16[2,512,512]{2,1,0:T(8,128)(2,1)} %bitcast.8, bf16[2,512,512]{2,1,0:T(8,128)(2,1)} %bitcast.9, bf16[512,512]{1,0:T(8,128)(2,1)} %rm_h.1, bf16[512,512]{1,0:T(8,128)(2,1)} %cm_h.1, ...), custom_call_target="tpu_custom_call" | custom-call | tf_op jit(solution)/shard_map/monarch_backward/pallas_call | solution.py:321
  235.8 0.0 copy-start
  235.8 3.2 %copy.11 = bf16[2048,512]{1,0:T(8,128)(2,1)} copy(bf16[2048,512]{1,0:T(8,128)(2,1)} %bitcast.5) | data formatting | bytes 4194304
  239.0 0.0 copy-done
  239.0 1.3 copy.12
Async XLA Ops:
  235.8 3.2 %copy-start = (bf16[512,4,512]{2,1,0:T(4,128)(2,1)S(1)}, bf16[512,4,512]{2,1,0:T(4,128)(2,1)}, u32[]{:S(2)}) copy-start(bf16[512,4,512]{2,1,0:T(4,128)(2,1)} %get-tuple-element.9) | copy-start | bytes 6291460

commit v4 on v3

--- a/solution.py
+++ b/solution.py
@@ -240,12 +240,13 @@
         store_gk = pltpu.make_async_copy(raw, gk_h, gk_sem)
         store_gk.start()
 
-        def scatter(i):
+        def scatter(i, b):
+            cols = pl.ds(pl.multiple_of(b * lanes, lanes), lanes)
             return pltpu.make_async_remote_copy(
-                src_ref=rss.at[i],
-                dst_ref=rsr.at[i],
-                send_sem=rs_s.at[i],
-                recv_sem=rs_r.at[i],
+                src_ref=rss.at[i, :, cols],
+                dst_ref=rsr.at[i, :, cols],
+                send_sem=rs_s.at[i, b],
+                recv_sem=rs_r.at[i, b],
                 device_id={"chan": other},
                 device_id_type=MESH,
             )
@@ -254,8 +255,13 @@
             return pltpu.make_async_copy(out.at[i], gt_h.at[i], gt_sem.at[i])
 
         def finish(i):
-            scatter(i).wait_recv()
-            out[i] = (own[i] + rsr[i].astype(F32)).astype(BF16)
+            def add(b, inner):
+                cols = pl.ds(pl.multiple_of(b * lanes, lanes), lanes)
+                scatter(i, b).wait_recv()
+                out[i, :, cols] = (own[i, :, cols] + rsr[i, :, cols].astype(F32)).astype(BF16)
+                return inner
+
+            lax.fori_loop(0, local // lanes, add, 0)
             store(i).start()
 
         def rows_step(i, carry):
@@ -278,10 +284,10 @@
                 rss[i, :, rows] = (
                     mm_nt(tok[i], wg[other, rows, :]) + mm_nt(tokp[i], wv[other, rows, :])
                 ).astype(BF16)
+                scatter(i, b).start()
                 return inner
 
             lax.fori_loop(0, local // lanes, away, 0)
-            scatter(i).start()
 
             def home(b, inner):
                 rows = pl.ds(pl.multiple_of(b * lanes, lanes), lanes)
@@ -303,7 +309,8 @@
             gather(i).wait_send()
             sent(sa, i, a_s)
             sent(sb, i, b_s)
-            scatter(i).wait_send()
+            for b in range(local // lanes):
+                scatter(i, b).wait_send()
             store(i).wait()
         store_gk.wait()
 
@@ -342,7 +349,9 @@
             pltpu.VMEM(wide, F32), pltpu.VMEM(wide, BF16),
             dma((7,)), dma((2 * Q,)),
             dma((Q,)), dma((Q,)), dma((Q,)), dma((Q, n // BLK)),
-            *[dma((Q,)) for _ in range(5)],
+            dma((Q,)), dma((Q,)),
+            dma((Q, 2)), dma((Q, 2)),
+            dma((Q,)),
             dma,
         ],
         compiler_params=pltpu.CompilerParams(

time: 240 us -> 240 us (level)
  no operation moved by 1% of the time
where the time goes in v4:
time: 240 us
  Pallas kernels  235 us (98%)
  local copies, waits for them, and re-layouts  4.52 us (2%)
    pallas_call x1, Pallas kernels, body(): pl.pallas_call(make_kernel(n, side, local), name='monarch_backward', out_...  235 us

profile of v4, /device:TPU:14, one launch (start us, length us, event | category | flops | bytes accessed | tf_op | source)
XLA Modules:
  0.0 239.9 jit_solution(5940245187921402994)
XLA Ops:
  0.6 234.7 %monarch_backward.1 = (bf16[4,512,512]{2,1,0:T(8,128)(2,1)}, bf16[512,4,512]{2,1,0:T(4,128)(2,1)}) custom-call(bf16[4,512,512]{2,1,0:T(8,128)(2,1)} %bitcast.6, bf16[2,512,512]{2,1,0:T(8,128)(2,1)} %bitcast.8, bf16[2,512,512]{2,1,0:T(8,128)(2,1)} %bitcast.9, bf16[512,512]{1,0:T(8,128)(2,1)} %rm_h.1, bf16[512,512]{1,0:T(8,128)(2,1)} %cm_h.1, ...), custom_call_target="tpu_custom_call" | custom-call | tf_op jit(solution)/shard_map/monarch_backward/pallas_call | solution.py:328
  235.4 0.0 copy-start
  235.4 3.2 %copy.11 = bf16[2048,512]{1,0:T(8,128)(2,1)} copy(bf16[2048,512]{1,0:T(8,128)(2,1)} %bitcast.5) | data formatting | bytes 4194304
  238.6 0.0 copy-done
  238.6 1.3 copy.12
Async XLA Ops:
  235.4 3.2 %copy-start = (bf16[512,4,512]{2,1,0:T(4,128)(2,1)S(1)}, bf16[512,4,512]{2,1,0:T(4,128)(2,1)}, u32[]{:S(2)}) copy-start(bf16[512,4,512]{2,1,0:T(4,128)(2,1)} %get-tuple-element.9) | copy-start | bytes 6291460
